TPU v7x, 256 devices: a whole 4x4x8 slice. The times are simulated.
256 devices in a mesh: scen: 16 (over z, core), clus: 16 (over y, x).
Axes of the slice: x: 4, y: 4, z: 8, core: 2. Of those that a mesh axis runs over, the one named last changes fastest.
Arguments:
- duals: bfloat16 [16384, 2, 128], P(('scen', 'clus')), may hold values from -6 to 6
- blocks: bfloat16 [16384, 2, 128, 128], P(('scen', 'clus')), may hold values from -0.5 to 0.5
- prob: float32 [16384], P(('scen', 'clus')), may hold values from 0.25 to 4
- cluster_map: int32 [16384], P(('scen', 'clus')), may hold values from 0 to 15
- block_cols: int32 [16384, 2], P(('scen', 'clus')), may hold values from 0 to 255
- counts: int32 [256], P(('scen', 'clus')), may hold values from 16 to 64, as said below
- cut_owner_rows: int32 [256], replicated, may hold values from 0 to 255, as said below
Outputs:
- master_cuts: float32 [256, 32768], P('clus', 'scen')
Inputs may be any that keep to these rules, and one draw needn't show every extreme that they name: counts of live slots, one device holding 64 live slots in every draw. A permutation of the master cut rows; of the cuts k = i * 16 to (i + 1) * 16 - 1 at most 1 have cut_owner_rows[k] in e * 16 to (e + 1) * 16 - 1, for any i and e, and 1 is reached.
All inputs are finite; a program needn't handle non-finite values.
Results may differ from a plain program's by a relative error of at most 0.0029.
Values sent between devices are 32-bit elements; how exact they have to be, the bound alone decides.
A program may use at most 64 MiB of HBM per device.

v0:
```python
import jax
import jax.numpy as jnp
from jax import lax
from jax.sharding import PartitionSpec as P

N1 = 32768
KC = 16


def body(duals, blocks, prob, cluster_map, block_cols, counts, cut_owner_rows):
    slots = prob.shape[0]
    width = blocks.shape[-1]
    col_blocks = N1 // width
    cluster_position = lax.axis_index("clus")
    own_blocks = col_blocks // lax.axis_size("scen")
    columns = own_blocks * width
    live = jnp.arange(slots, dtype=jnp.int32) < counts[0]
    weight = jnp.where(live, prob, jnp.float32(0.0))
    weighted_duals = (weight[:, None, None] * duals.astype(jnp.float32)).astype(jnp.bfloat16)
    dual_products = jnp.einsum(
        "plqv,plq->plv", blocks, weighted_duals, preferred_element_type=jnp.float32
    )
    dual_products = dual_products.reshape(-1, width)
    keys = (cluster_map[:, None] * col_blocks + block_cols).reshape(-1)
    clus_part = keys // col_blocks
    col_part = keys % col_blocks
    valid = (col_part >= 0) & (col_part < lax.axis_size("scen") * own_blocks)
    target = jnp.where(valid, col_part * KC + clus_part, -1)
    onehot = (
        target[None, :]
        == jnp.arange(lax.axis_size("scen") * own_blocks * KC, dtype=jnp.int32)[:, None]
    ).astype(jnp.float32)
    summed = jnp.dot(
        onehot, dual_products, precision=lax.Precision.HIGHEST, preferred_element_type=jnp.float32
    )
    probability_shares = lax.psum_scatter(
        summed.reshape(lax.axis_size("scen") * own_blocks, KC, width),
        "scen",
        scatter_dimension=0,
        tiled=True,
    )
    reduced = jnp.transpose(probability_shares, (1, 0, 2)).reshape(KC, columns)
    owners = cut_owner_rows - cluster_position * KC
    onehot = (owners[None, :] == jnp.arange(KC, dtype=jnp.int32)[:, None]).astype(jnp.float32)
    return jnp.dot(
        onehot,
        lax.all_gather(reduced, "clus", axis=0, tiled=True),
        precision=lax.Precision.HIGHEST,
        preferred_element_type=jnp.float32,
    )


def solution(mesh):
    placed = (
        P(("scen", "clus"), None, None),
        P(("scen", "clus"), None, None, None),
        P(("scen", "clus")),
        P(("scen", "clus")),
        P(("scen", "clus"), None),
        P(("scen", "clus")),
        P(),
    )
    return jax.shard_map(
        body, mesh=mesh, in_specs=placed, out_specs=P("clus", "scen"), check_vma=False
    )
```

profile of v0, /device:TPU:1, one launch (start us, length us, event | category | flops | bytes accessed | tf_op | source)
XLA Modules:
  0.0 139.5 jit_solution(1167170672462910426)
XLA Ops:
  6.5 0.0 reduce-scatter.2.cloned.1.call-start
  7.2 0.7 broadcast_multiply_fusion
  7.9 0.7 broadcast_add_fusion
  8.5 0.1 copy.9
  8.6 0.1 reshape.86
  8.8 0.7 compare_select_fusion
  9.5 0.9 fusion.6
  10.3 3.4 %fusion.4 = f32[64,2,1,128]{3,2,1,0:T(1,128)S(1)} fusion(bf16[64,2,128,128]{3,2,1,0:T(8,128)(2,1)} %param.8, bf16[64,2,128,1]{2,1,0,3:T(2,128)(2,1)S(1)} %fusion.6), kind=kOutput, calls=%fused_computation.5 | convolution fusion | flops 4194304 | bytes 4292608 | tf_op jit(solution)/shard_map/plqv,plq->plv/dot_general | solution.py:20
  13.7 0.0 copy-start
  13.7 2.5 %fusion = f32[256,16,128]{2,0,1:T(8,128)} fusion(f32[128,128,1]{1,0,2:T(8,128)S(1)} %bitcast.19, s32[256,16]{0,1:T(8,128)S(1)} %multiply_add_fusion, s32[128]{0:T(128)S(1)} %and_select_fusion.1), kind=kOutput, calls=%fused_computation | convolution fusion | flops 805830656 | bytes 2179584 | tf_op jit(solution)/shard_map/dot_general | solution.py:33
  16.2 0.0 reduce-scatter.2.cloned.1.call-update
  16.3 0.0 all-gather.2.cloned.1.call-start
  16.3 60.2 %reduce-scatter.2.cloned.1.call-done = f32[16,16,128]{2,0,1:T(8,128)} async-done(((f32[256,16,128]{2,0,1:T(8,128)}), f32[16,16,128]{2,0,1:T(8,128)}) %reduce-scatter.2.cloned.1.call-update) | async-done | bytes 131088 | tf_op jit(solution)/shard_map/reduce_scatter | solution.py:36
  76.6 1.6 %copy.16 = f32[2,8,16,128]{3,1,2,0:T(8,128)} copy(f32[2,8,16,128]{3,2,1,0:T(8,128)} %bitcast.20) | data formatting | bytes 262144
  78.2 0.0 all-gather.2.cloned.1.call-update
  78.2 0.0 copy-done
  78.2 51.4 %all-gather.2.cloned.1.call-done = f32[256,2048]{1,0:T(8,128)} async-done(((f32[16,2048]{1,0:T(8,128)}), f32[256,2048]{1,0:T(8,128)}) %all-gather.2.cloned.1.call-update) | async-done | bytes 2097168 | tf_op jit(solution)/shard_map/all_gather | solution.py:47
  129.6 3.0 %fusion.7 = f32[16,2048]{1,0:T(8,128)} fusion(f32[256,2048]{1,0:T(8,128)} %all-gather.2.cloned.1.call-done, s32[256]{0:T(256)S(1)} %broadcast_subtract_fusion), kind=kOutput, calls=%fused_computation.11 | convolution fusion | flops 100667392 | bytes 2229248 | tf_op jit(solution)/shard_map/dot_general | solution.py:45
  (3 shorter events, 0.0 us)
Async XLA Ops:
  6.5 70.0 %reduce-scatter.2.cloned.1.call-start = ((), (), s32[]{:S(2)}) async-start(), calls=%async_computation.1 | async-start | bytes 2228224 | tf_op jit(solution)/shard_map/reduce_scatter | solution.py:36
  13.7 64.5 %copy-start = (s32[256]{0:T(256)S(1)}, s32[256]{0:T(256)}, u32[]{:S(2)}) copy-start(s32[256]{0:T(256)} %param.13) | copy-start | bytes 3076
  16.3 113.3 %all-gather.2.cloned.1.call-start = ((), (), s32[]{:S(2)}) async-start(), calls=%async_computation.2 | async-start | bytes 2228224 | tf_op jit(solution)/shard_map/all_gather | solution.py:47
Sparse Core Ops, SparseCore 0:
  16.4 60.1 reduce-scatter.1
  79.0 50.5 all-gather.1
where the time goes:
time: 140 us; the launch traced here: 139 us
  waiting for transfers between devices  112 us (80%)
  between operations  14.1 us (10%)
  matrix products  8.91 us (6%)
  other arithmetic  2.91 us (2%)
  local copies, waits for them, and re-layouts  1.84 us (1%)
    reduce_scatter x1, waiting for transfers between devices, body(): lax.psum_scatter(summed.reshape(lax.axis_size('scen') * own_blocks, KC, w...  60.2 us
    all_gather x1, waiting for transfers between devices, body(): lax.all_gather(reduced, 'clus', axis=0, tiled=True)  51.4 us
    dot_general x1, matrix products, body(): jnp.einsum('plqv,plq->plv', blocks, weighted_duals, preferred_element_typ...  3.37 us
    dot_general x1, matrix products, body(): jnp.dot(onehot, lax.all_gather(reduced, 'clus', axis=0, tiled=True), prec...  3.02 us
  transfers between devices with their start and end apart: 2, of which 2 were waited for; matrix products, arithmetic and copies ran while one was open for 0% of the time, Pallas kernels for 0%

commit v1 on v0

--- a/solution.py
+++ b/solution.py
@@ -2,12 +2,25 @@
 import jax.numpy as jnp
 from jax import lax
 from jax.sharding import PartitionSpec as P
+from jax.lax import all_to_all, axis_size
 
 N1 = 32768
 KC = 16
 
 
 def body(duals, blocks, prob, cluster_map, block_cols, counts, cut_owner_rows):
+
+    def _list_strings(vector, axis_key, k_dim=0):
+        return jnp.concatenate(
+            all_to_all(
+                jnp.stack(tuple((vector for _ in range(axis_size(axis_key)))), axis=0),
+                axis_key,
+                split_axis=0,
+                concat_axis=0,
+            ),
+            k_dim,
+        )
+
     slots = prob.shape[0]
     width = blocks.shape[-1]
     col_blocks = N1 // width
@@ -44,7 +57,7 @@
     onehot = (owners[None, :] == jnp.arange(KC, dtype=jnp.int32)[:, None]).astype(jnp.float32)
     return jnp.dot(
         onehot,
-        lax.all_gather(reduced, "clus", axis=0, tiled=True),
+        _list_strings(reduced, "clus"),
         precision=lax.Precision.HIGHEST,
         preferred_element_type=jnp.float32,
     )

time: 140 us -> 125 us (0.89)
  the two profiles are of different devices: /device:TPU:1 before, /device:TPU:225 now
where the time goes in v1:
time: 125 us
  waiting for transfers between devices  91.5 us (73%)
  between operations  14.1 us (11%)
  matrix products  7.3 us (6%)
  starting transfers between devices  6.64 us (5%)
  other arithmetic  2.91 us (2%)
  local copies, waits for them, and re-layouts  2.76 us (2%)
    reduce_scatter x1, waiting for transfers between devices, body(): lax.psum_scatter(summed.reshape(lax.axis_size('scen') * own_blocks, KC, w...  57.3 us
    all_to_all x1, waiting for transfers between devices, _list_strings(): all_to_all(jnp.stack(tuple((vector for _ in range(axis_size(axis_key)))),...  34.2 us
    all_to_all x1, starting transfers between devices, _list_strings(): all_to_all(jnp.stack(tuple((vector for _ in range(axis_size(axis_key)))),...  6.64 us
    dot_general x1, matrix products, body(): jnp.einsum('plqv,plq->plv', blocks, weighted_duals, preferred_element_typ...  3.37 us
  transfers between devices with their start and end apart: 2, of which 2 were waited for; matrix products, arithmetic and copies ran while one was open for 0% of the time, Pallas kernels for 0%

profile of v1, /device:TPU:225, one launch (start us, length us, event | category | flops | bytes accessed | tf_op | source)
XLA Modules:
  0.0 125.2 jit_solution(16346586638665970043)
XLA Ops:
  6.5 0.0 reduce-scatter.2.cloned.1.call-start
  7.2 0.7 broadcast_multiply_fusion
  7.9 0.7 broadcast_add_fusion
  8.5 0.1 copy.9
  8.6 0.1 reshape.88
  8.8 0.7 compare_select_fusion
  9.5 0.9 fusion.6
  10.3 3.4 %fusion.4 = f32[64,2,1,128]{3,2,1,0:T(1,128)S(1)} fusion(bf16[64,2,128,128]{3,2,1,0:T(8,128)(2,1)} %param.8, bf16[64,2,128,1]{2,1,0,3:T(2,128)(2,1)S(1)} %fusion.6), kind=kOutput, calls=%fused_computation.5 | convolution fusion | flops 4194304 | bytes 4292608 | tf_op jit(solution)/shard_map/plqv,plq->plv/dot_general | solution.py:33
  13.7 2.5 %fusion = f32[256,16,128]{2,0,1:T(8,128)} fusion(f32[128,128,1]{1,0,2:T(8,128)S(1)} %bitcast.21, s32[256,16]{0,1:T(8,128)S(1)} %multiply_add_fusion, s32[128]{0:T(128)S(1)} %and_select_fusion.1), kind=kOutput, calls=%fused_computation | convolution fusion | flops 805830656 | bytes 2179584 | tf_op jit(solution)/shard_map/dot_general | solution.py:46
  16.2 0.0 reduce-scatter.2.cloned.1.call-update
  16.2 57.3 %reduce-scatter.2.cloned.1.call-done = f32[16,16,128]{2,0,1:T(8,128)} async-done(((f32[256,16,128]{2,0,1:T(8,128)}), f32[16,16,128]{2,0,1:T(8,128)}) %reduce-scatter.2.cloned.1.call-update) | async-done | bytes 131088 | tf_op jit(solution)/shard_map/reduce_scatter | solution.py:49
  73.5 0.9 copy.16
  74.4 1.6 %stack.3 = f32[16,16,2048]{2,1,0:T(8,128)} broadcast(f32[16,2048]{1,0:T(8,128)S(1)} %bitcast.20), dimensions={1,2} | broadcast | bytes 2228224 | tf_op jit(solution)/shard_map/stack | solution.py:16
  76.0 0.0 copy-start
  76.0 6.6 %all-to-all-start = ((f32[16,16,2048]{2,1,0:T(8,128)}), f32[16,16,2048]{2,1,0:T(8,128)S(1)}, u32[]{:S(2)}, u32[]{:S(2)}) async-start(f32[16,16,2048]{2,1,0:T(8,128)} %stack.3), calls=%async_computation.1 | async-start | bytes 4194304 | tf_op jit(solution)/shard_map/all_to_all | solution.py:15
  82.7 0.0 copy-done
  82.7 34.2 %all-to-all-done = f32[16,16,2048]{2,1,0:T(8,128)S(1)} async-done(((f32[16,16,2048]{2,1,0:T(8,128)}), f32[16,16,2048]{2,1,0:T(8,128)S(1)}, u32[]{:S(2)}, u32[]{:S(2)}) %all-to-all-start) | async-done | bytes 2097184 | tf_op jit(solution)/shard_map/all_to_all | solution.py:15
  116.9 1.5 %fusion.7 = f32[16,2048]{1,0:T(8,128)} fusion(f32[256,2048]{1,0:T(8,128)S(1)} %bitcast.19, s32[256]{0:T(256)S(1)} %broadcast_subtract_fusion), kind=kOutput, calls=%fused_computation.11 | convolution fusion | flops 100667392 | bytes 2229248 | tf_op jit(solution)/shard_map/dot_general | solution.py:58
  (3 shorter events, 0.0 us)
Async XLA Ops:
  6.5 67.0 %reduce-scatter.2.cloned.1.call-start = ((), (), s32[]{:S(2)}) async-start(), calls=%async_computation.2 | async-start | bytes 2228224 | tf_op jit(solution)/shard_map/reduce_scatter | solution.py:49
  76.0 6.7 %copy-start = (s32[256]{0:T(256)S(1)}, s32[256]{0:T(256)}, u32[]{:S(2)}) copy-start(s32[256]{0:T(256)} %param.13) | copy-start | bytes 3076
  76.0 40.9 %all-to-all-start = ((f32[16,16,2048]{2,1,0:T(8,128)}), f32[16,16,2048]{2,1,0:T(8,128)S(1)}, u32[]{:S(2)}, u32[]{:S(2)}) async-start(f32[16,16,2048]{2,1,0:T(8,128)} %stack.3), calls=%async_computation.1 | async-start | bytes 4194304 | tf_op jit(solution)/shard_map/all_to_all | solution.py:15
Sparse Core Ops, SparseCore 0:
  16.3 57.0 reduce-scatter.1
